TPU v7x, 32 devices: a whole 2x2x4 slice. The times are simulated.
32 devices in a mesh: req: 2 (over x), ctx: 4 (over y, core), tp: 4 (over z).
Axes of the slice: x: 2, y: 2, z: 4, core: 2. Of those that a mesh axis runs over, the one named last changes fastest.
Arguments:
- queries: bfloat16 [512, 16, 128], P('req', 'tp'), may hold values from -5 to 5
- new_keys: bfloat16 [512, 4, 128], P('req', 'tp'), may hold values from -5 to 5
- new_values: bfloat16 [512, 4, 128], P('req', 'tp'), may hold values from -24 to 24
- cache_keys: bfloat16 [2, 8192, 4, 128], P('req', 'ctx', 'tp'), may hold values from -5 to 5
- cache_values: bfloat16 [2, 8192, 4, 128], P('req', 'ctx', 'tp'), may hold values from -24 to 24
- cache_lengths: int32 [2], replicated, may hold values from 1 to 8192, as said below
- residual: bfloat16 [512, 2048], P(('req', 'ctx'), 'tp'), may hold values from -24 to 24
- out_weight: bfloat16 [2048, 2048], P('tp', 'ctx'), may hold values from -0.52734375 to 0.52734375
- norm_gain: float32 [2048], replicated, may hold values from 0.1 to 1.9
- expert_ids: int32 [512, 6], P(('req', 'ctx')), may hold values from 0 to 63, all different within a row; in each aligned block of 64 rows (0 to 63, 64 to 127, ...) at most 8 rows name the same one
- gate_weights: float32 [512, 6], P(('req', 'ctx')), may hold values from 0.1 to 1
- w_gate: bfloat16 [64, 2048, 1408], P('req', 'ctx', 'tp'), may hold values from -0.125 to 0.125
- w_up: bfloat16 [64, 2048, 1408], P('req', 'ctx', 'tp'), may hold values from -0.125 to 0.125
- w_down: bfloat16 [64, 1408, 2048], P('req', 'tp', 'ctx'), may hold values from -0.15625 to 0.15625
Outputs:
- layer_out: bfloat16 [512, 2048], P(('req', 'ctx'), 'tp')
Inputs may be any that keep to these rules, and one draw needn't show every extreme that they name: `cache_lengths`: the longest cached length equals 8192. `expert_ids`: within each aligned block of 64 tokens no expert is named by more than 8 routes, a bound that some block reaches.
All inputs are finite; a program needn't handle non-finite values.
Results may differ from a plain program's by a relative error of at most 0.006.
Values may be sent and summed in bfloat16 or wider, within the bound.
A program may use at most 384 MiB of HBM per device.

v0:
```python
import jax
import jax.numpy as jnp
from jax import lax
from jax.sharding import PartitionSpec as P

TOP = 6
CAP = 8
MASKED = -1e30


def attention_part(queries, new_keys, new_values, cache_keys, cache_values, length):
    ctx_pos, ctx_count = (lax.axis_index("ctx"), lax.axis_size("ctx"))
    tok_dev, heads, hd = queries.shape
    cache_dev = cache_keys.shape[1]
    block = tok_dev // ctx_count
    rows = heads * block
    q = queries.reshape(ctx_count, block, heads, hd).transpose(0, 2, 1, 3)
    q = q.reshape(ctx_count * rows, hd)
    keys = jnp.concatenate([cache_keys[0, :, 0, :], new_keys[:, 0, :]], 0)
    values = jnp.concatenate([cache_values[0, :, 0, :], new_values[:, 0, :]], 0)
    scores = jnp.dot(keys, q.T, preferred_element_type=jnp.float32) * hd ** (-0.5)
    key_at = jnp.arange(cache_dev + tok_dev, dtype=jnp.int32)[:, None]
    row_at = jnp.arange(ctx_count * rows, dtype=jnp.int32)[None, :]
    token = row_at // rows * block + row_at % block
    valid = jnp.where(
        key_at < cache_dev,
        ctx_pos * cache_dev + key_at < length,
        jnp.logical_and(ctx_pos == ctx_count - 1, key_at - cache_dev <= token),
    )
    scores = jnp.where(valid, scores, MASKED)
    top = jnp.max(scores, 0, keepdims=True)
    weights = jnp.where(valid, jnp.exp(scores - top), 0.0)
    total = jnp.sum(weights, 0, keepdims=True)
    sums = lax.dot_general(
        values,
        weights.astype(jnp.bfloat16),
        (((0,), (0,)), ((), ())),
        preferred_element_type=jnp.float32,
    )
    pack = jnp.concatenate([sums, top, total, jnp.zeros((6, ctx_count * rows), jnp.float32)], 0)
    return pack.reshape(hd + 8, ctx_count, rows).transpose(1, 0, 2)


def merge(packs, hd, heads):
    top = jnp.max(packs[:, hd : hd + 1], 0)
    factor = jnp.exp(packs[:, hd : hd + 1] - top)
    total = jnp.sum(factor * packs[:, hd + 1 : hd + 2], 0)
    out = (jnp.sum(factor * packs[:, :hd], 0) / total).astype(jnp.bfloat16)
    block = out.shape[1] // heads
    return out.reshape(hd, heads, block).transpose(2, 1, 0).reshape(block, heads * hd)


def route_tables(expert_ids, gate_weights, exp_dev):
    block = expert_ids.shape[0]
    both = jnp.concatenate([expert_ids.astype(jnp.float32), gate_weights], 1)
    both = lax.all_gather(both, ("req", "ctx"))
    blocks = both.shape[0]
    ids = both[:, :, :TOP].astype(jnp.int32)
    gates = both[:, :, TOP:]
    first = lax.axis_index("req") * exp_dev
    experts = first + jnp.arange(exp_dev, dtype=jnp.int32)
    hits = ids[:, :, :, None] == experts
    gate_at = jnp.sum(jnp.where(hits, gates[..., None], 0.0), 2)
    hit = jnp.any(hits, 2)
    earlier = jnp.tril(jnp.ones((block, block), jnp.bfloat16), -1)
    rank = jnp.einsum(
        "ij,bje->bie", earlier, hit.astype(jnp.bfloat16), preferred_element_type=jnp.float32
    )
    code = jnp.arange(blocks, dtype=jnp.int32)[:, None, None] * CAP + rank.astype(jnp.int32)
    code = jnp.where(hit, code, -1)
    flat = (blocks * block, exp_dev)
    return (code.reshape(flat).T, gate_at.reshape(flat).T)


def body(
    queries,
    new_keys,
    new_values,
    cache_keys,
    cache_values,
    cache_lengths,
    residual,
    out_weight,
    norm_gain,
    expert_ids,
    gate_weights,
    w_gate,
    w_up,
    w_down,
):
    ctx_pos, tp_pos, req_pos = (lax.axis_index(a) for a in ("ctx", "tp", "req"))
    ctx_count, req_count = (lax.axis_size("ctx"), lax.axis_size("req"))
    tok_dev, heads, hd = queries.shape
    block, share = residual.shape
    exp_dev = w_gate.shape[0]
    slots = req_count * ctx_count * CAP
    length = lax.dynamic_index_in_dim(cache_lengths, req_pos, 0, keepdims=False)
    code, gate_at = route_tables(expert_ids, gate_weights, exp_dev)
    swap = [
        (a * ctx_count + b, b * ctx_count + a) for a in range(ctx_count) for b in range(ctx_count)
    ]
    residual_t = lax.ppermute(residual, ("ctx", "tp"), swap)
    packs = attention_part(queries, new_keys, new_values, cache_keys, cache_values, length)
    packs = lax.all_to_all(packs, "ctx", 0, 0, tiled=True)
    attended = merge(packs, hd, heads)
    attended = lax.all_gather(attended, "ctx", tiled=True)
    part = jnp.dot(attended, out_weight, preferred_element_type=jnp.float32)
    part = part.reshape(-1, block, share)
    part = lax.all_to_all(part, "tp", 0, 0, tiled=True)
    hidden = jnp.sum(part, 0) + residual_t.astype(jnp.float32)
    squares = jnp.sum(hidden * hidden, 1)
    gain = lax.dynamic_slice_in_dim(norm_gain, ctx_pos * share, share, 0)
    scaled = (hidden * gain).astype(jnp.bfloat16)
    squares = lax.psum(squares, "ctx")
    factor = lax.rsqrt(squares / norm_gain.shape[0] + 1e-06)
    factor = lax.all_gather(factor, ("req", "tp"), tiled=True)
    scaled = lax.all_gather(scaled, ("req", "tp"), tiled=True)
    pick = code[:, None, :] == jnp.arange(slots, dtype=jnp.int32)[None, :, None]
    row_factor = jnp.sum(jnp.where(pick, factor, 0.0), -1, keepdims=True)
    row_gate = jnp.sum(jnp.where(pick, gate_at[:, None, :], 0.0), -1, keepdims=True)
    pick = pick.astype(jnp.bfloat16)
    rows = jnp.einsum("est,td->esd", pick, scaled, preferred_element_type=jnp.bfloat16)
    gate = jnp.einsum("esd,edf->esf", rows, w_gate, preferred_element_type=jnp.float32)
    up = jnp.einsum("esd,edf->esf", rows, w_up, preferred_element_type=jnp.float32)
    both = jnp.stack([gate, up], 2).astype(jnp.bfloat16)
    both = both.reshape(ctx_count, exp_dev * slots // ctx_count, 2, -1)
    both = lax.all_to_all(both, "ctx", 0, 0, tiled=True)
    both = both.astype(jnp.float32).sum(0)
    per = exp_dev * slots // ctx_count
    mine = lax.dynamic_slice_in_dim(row_factor.reshape(-1, 1), ctx_pos * per, per, 0)
    inner = (jax.nn.silu(both[:, 0] * mine) * (both[:, 1] * mine)).astype(jnp.bfloat16)
    inner = lax.all_gather(inner, "ctx", tiled=True).reshape(exp_dev, slots, -1)
    down = jnp.einsum("esf,efd->esd", inner, w_down, preferred_element_type=jnp.float32)
    down = (down * row_gate).astype(jnp.bfloat16)
    mixed = jnp.einsum("est,esd->td", pick, down, preferred_element_type=jnp.float32)
    mixed = mixed.astype(jnp.bfloat16).reshape(-1, block, share)
    mixed = lax.all_to_all(mixed, ("req", "tp"), 0, 0, tiled=True)
    out = hidden + jnp.sum(mixed.astype(jnp.float32), 0)
    return lax.ppermute(out.astype(jnp.bfloat16), ("ctx", "tp"), swap)


def solution(mesh):
    in_specs = (
        P("req", "tp", None),
        P("req", "tp", None),
        P("req", "tp", None),
        P("req", "ctx", "tp", None),
        P("req", "ctx", "tp", None),
        P(),
        P(("req", "ctx"), "tp"),
        P("tp", "ctx"),
        P(),
        P(("req", "ctx"), None),
        P(("req", "ctx"), None),
        P("req", "ctx", "tp"),
        P("req", "ctx", "tp"),
        P("req", "tp", "ctx"),
    )
    out_specs = P(("req", "ctx"), "tp")
    return jax.shard_map(body, mesh=mesh, in_specs=in_specs, out_specs=out_specs, check_vma=False)
```

profile of v0, /device:TPU:4, one launch (start us, length us, event | category | flops | bytes accessed | tf_op | source)
XLA Modules:
  0.0 254.7 jit_solution(7631431469196999747)
XLA Ops:
  6.6 1.0 copy.55
  7.6 1.2 dynamic_slice.10
  8.9 0.7 add_compare_fusion
  9.5 6.5 %fusion = (f32[1024]{0:T(1024)S(1)}, f32[2304,1024]{1,0:T(8,128)S(1)}) fusion(s32[1024]{0:T(1024)S(1)} %fusion.38, s32[2304]{0:T(1024)S(1)} %iota_add_fusion, pred[2304]{0:T(1024)(128)(4,1)S(1)} %get-tuple-element.17, pred[2304]{0:T(1024)(128)(4,1)S(1)} %get-tuple-element.18, pred[]{:T(512)S(6)} %eq.16, bf16[1024,128]{1,0:T(8,128)(2,1)S(1)} %bitcast.83, ...), kind=kOutput, calls=%fused_computation.3 | convolution fusion | flops 619314176 | bytes 10311169 | tf_op jit(solution)/shard_map/dot_general | solution.py:21
  16.0 0.0 copy-start.12
  16.0 0.0 copy-start.13
  16.0 4.7 %fusion.1 = f32[1024]{0:T(1024)S(1)} fusion(f32[2304,1024]{1,0:T(8,128)S(1)} %get-tuple-element.16, f32[1024]{0:T(1024)S(1)} %get-tuple-element.15, s32[1024]{0:T(1024)S(1)} %fusion.38, s32[2304]{0:T(1024)S(1)} %iota_add_fusion, pred[2304]{0:T(1024)(128)(4,1)S(1)} %get-tuple-element.17, pred[2304]{0:T(1024)(128)(4,1)S(1)} %get-tuple-element.18, pred[]{:T(512)S(6)} %eq.16), kind=kLoop, calls=%fused_computation.5 | loop fusion | flops 18873344 | bytes 9463297 | tf_op jit(solution)/shard_map/reduce_sum | solution.py:33
  20.8 0.0 copy-start.14
  20.8 0.0 copy-start.10
  20.8 0.0 copy-start.11
  20.8 4.0 %fusion.3 = f32[128,1024]{1,0:T(8,128)S(1)} fusion(f32[2304,1024]{1,0:T(8,128)S(1)} %get-tuple-element.16, f32[1024]{0:T(1024)S(1)} %get-tuple-element.15, s32[1024]{0:T(1024)S(1)} %fusion.38, s32[2304]{0:T(1024)S(1)} %iota_add_fusion, pred[2304]{0:T(1024)(128)(4,1)S(1)} %get-tuple-element.17, pred[2304]{0:T(1024)(128)(4,1)S(1)} %get-tuple-element.18, ...), kind=kOutput, calls=%fused_computation.7 | convolution fusion | flops 624033792 | bytes 10573313 | tf_op jit(solution)/shard_map/dot_general | solution.py:34
  24.9 0.1 pad.7.clone
  25.0 0.9 maximum_bitcast_fusion
  25.9 3.5 %all-to-all-start = ((f32[4,136,256]{2,1,0:T(8,128)}), f32[4,136,256]{2,1,0:T(8,128)S(1)}, u32[]{:S(2)}, u32[]{:S(2)}) async-start(f32[4,136,256]{2,1,0:T(8,128)} %maximum_bitcast_fusion), calls=%async_computation | async-start | bytes 1114112 | tf_op jit(solution)/shard_map/all_to_all | solution.py:104
  29.4 4.4 %collective-permute-start = (bf16[64,512]{1,0:T(8,128)(2,1)S(1)}, bf16[64,512]{1,0:T(8,128)(2,1)S(1)}, u32[]{:S(2)}, u32[]{:S(2)}) collective-permute-start(bf16[64,512]{1,0:T(8,128)(2,1)S(1)} %copy-done.14), channel_id=1, source_target_pairs={{0,0},{1,4},{2,8},{3,12},{4,1},{5,5},{6,9},{7,13},{8,2},{9,6},{10,... | collective-permute-start | bytes 196616 | tf_op jit(solution)/shard_map/ppermute | solution.py:102
  33.9 9.2 %all-gather.1 = f32[8,64,12]{1,2,0:T(8,128)S(1)} all-gather(f32[1,64,12]{1,2,0:T(8,128)S(1)} %maximum_bitcast_fusion.1), channel_id=2, replica_groups=mesh['req'=2,'ctx'=4,'tp'=4] {'req','ctx'}, dimensions={0}, use_global_device_ids=true | all-gather | bytes 27648 | tf_op jit(solution)/shard_map/all_gather | solution.py:56
  43.1 0.0 all-to-all-done
  43.2 0.1 copy.59
  43.3 0.1 div.31
  43.4 0.1 copy_bitcast_fusion.1
  43.5 5.8 %all_gather.18 = bf16[256,512]{1,0:T(8,128)(2,1)S(1)} all-gather(bf16[64,512]{1,0:T(8,128)(2,1)S(1)} %copy_bitcast_fusion.1), channel_id=1, replica_groups=mesh['req'=2,'ctx'=4,'tp'=4] {'ctx'}, dimensions={0}, use_global_device_ids=true | all-gather | bytes 327680 | tf_op jit(solution)/shard_map/all_gather | solution.py:106
  49.4 1.1 fusion.53
  50.5 5.1 %all-to-all-start.1 = ((f32[4,64,512]{2,1,0:T(8,128)}), f32[4,64,512]{2,1,0:T(8,128)S(1)}, u32[]{:S(2)}, u32[]{:S(2)}) async-start(f32[4,64,512]{2,1,0:T(8,128)} %bitcast.13), calls=%async_computation.1 | async-start | bytes 1048576 | tf_op jit(solution)/shard_map/all_to_all | solution.py:109
  55.6 0.6 fusion.52
  56.2 0.6 copy-done.2
  56.8 0.2 compare_reduce_fusion
  57.0 0.2 fusion.13
  57.2 0.1 copy.61
  57.3 0.1 reshape.144
  57.4 0.8 dynamic_slice.11
  58.2 12.4 %all-to-all-done.1 = f32[4,64,512]{2,1,0:T(8,128)S(1)} async-done(((f32[4,64,512]{2,1,0:T(8,128)}), f32[4,64,512]{2,1,0:T(8,128)S(1)}, u32[]{:S(2)}, u32[]{:S(2)}) %all-to-all-start.1) | async-done | bytes 524320 | tf_op jit(solution)/shard_map/all_to_all | solution.py:109
  70.7 0.0 collective-permute-done
  70.7 0.1 multiply_reduce_fusion
  70.8 32.5 %all_gather.21 = bf16[512,512]{1,0:T(8,128)(2,1)S(1)} all-gather(bf16[64,512]{1,0:T(8,128)(2,1)S(1)} %get-tuple-element.12), channel_id=1, replica_groups=mesh['req'=2,'ctx'=4,'tp'=4] {'req','tp'}, dimensions={0}, use_global_device_ids=true | all-gather | bytes 589824 | tf_op jit(solution)/shard_map/all_gather | solution.py:117
  103.3 1.3 fusion.6
  104.6 8.6 %convolution_convert_fusion = bf16[32,64,352]{2,1,0:T(8,128)(2,1)} fusion(bf16[32,64,512]{2,1,0:T(8,128)(2,1)S(1)} %fusion.6, bf16[32,512,352]{1,2,0:T(8,128)(2,1)} %param.26), kind=kOutput, calls=%fused_computation.17 | convolution fusion | flops 738918400 | bytes 15073280 | tf_op jit(solution)/shard_map/esd,edf->esf/dot_general | solution.py:124
  113.2 2.5 copy.63
  115.7 8.6 %convolution_convert_fusion.1 = bf16[32,64,352]{2,1,0:T(8,128)(2,1)} fusion(bf16[32,64,512]{2,1,0:T(8,128)(2,1)S(1)} %fusion.6, bf16[32,512,352]{1,2,0:T(8,128)(2,1)} %param.25), kind=kOutput, calls=%fused_computation.18 | convolution fusion | flops 738918400 | bytes 15073280 | tf_op jit(solution)/shard_map/esd,edf->esf/dot_general | solution.py:123
  124.3 1.7 copy.62
  126.0 3.2 %pad_maximum_fusion = bf16[4,512,2,352]{1,3,2,0:T(8,128)(2,1)} fusion(bf16[4,512,1,352]{1,3,2,0:T(8,128)(2,1)} %copy.63, bf16[4,512,1,352]{1,3,2,0:T(8,128)(2,1)S(1)} %copy.62), kind=kLoop, calls=%fused_computation.14 | loop fusion | flops 1441792 | bytes 5767168 | tf_op jit(solution)/shard_map/stack | solution.py:125
  129.3 5.4 %all-to-all-start.2 = ((bf16[4,512,2,352]{1,3,2,0:T(8,128)(2,1)}), bf16[4,512,2,352]{1,3,2,0:T(8,128)(2,1)S(1)}, u32[]{:S(2)}, u32[]{:S(2)}) async-start(bf16[4,512,2,352]{1,3,2,0:T(8,128)(2,1)} %pad_maximum_fusion), calls=%async_computation.2 | async-start | bytes 5767168 | tf_op jit(solution)/shard_map/all_to_all | solution.py:127
  134.6 0.2 fusion.14
  134.8 0.1 copy.67
  134.9 0.1 reshape.146
  135.0 0.6 dynamic-slice
  136.3 33.5 %psum.7 = f32[64]{0:T(128)S(1)} all-reduce(f32[64]{0:T(128)S(1)} %get-tuple-element.11), channel_id=1, replica_groups=mesh['req'=2,'ctx'=4,'tp'=4] {'ctx'}, use_global_device_ids=true, to_apply=%region_9.10 | all-reduce | flops 64 | bytes 512 | tf_op jit(solution)/shard_map/psum | solution.py:114
  169.8 0.1 rsqrt_dynamic-update-slice_fusion
  169.9 18.9 %all-reduce = f32[512]{0:T(512)S(1)} all-reduce(f32[512]{0:T(512)S(1)} %rsqrt_dynamic-update-slice_fusion), channel_id=1, replica_groups=mesh['req'=2,'ctx'=4,'tp'=4] {'req','tp'}, use_global_device_ids=true, to_apply=%add | all-reduce | flops 512 | bytes 4096
  188.8 1.5 select_reduce_fusion
  190.3 0.1 reshape_broadcast_in_dim.3
  190.4 0.4 convert_reduce_fusion
  190.8 0.0 copy-start.6
  190.8 0.1 fusion.51
  190.9 0.3 copy.73
  191.2 0.3 copy.72
  191.5 1.0 fusion.16
  192.5 0.0 all-gather.4.cloned.1.call-update
  192.5 17.0 %all-gather.4.cloned.1.call-done = bf16[2048,352]{1,0:T(8,128)(2,1)} async-done(((bf16[512,352]{1,0:T(8,128)(2,1)}), bf16[2048,352]{1,0:T(8,128)(2,1)}) %all-gather.4.cloned.1.call-update) | async-done | bytes 1441808 | tf_op jit(solution)/shard_map/all_gather | solution.py:132
  209.5 8.2 %fusion.10 = bf16[512,512]{1,0:T(8,128)(2,1)S(1)} fusion(s32[32,512]{1,0:T(8,128)S(1)} %bitcast.86, bf16[32,64,352]{2,1,0:T(8,128)(2,1)} %bitcast.92, bf16[32,352,512]{2,1,0:T(8,128)(2,1)} %param.27, f32[32,64]{1,0:T(8,128)S(1)} %get-tuple-element.5), kind=kOutput, calls=%fused_computation.20 | convolution fusion | flops 1815347200 | bytes 13574144 | tf_op jit(solution)/shard_map/est,esd->td/dot_general | solution.py:135
  217.8 21.4 %all_to_all.20 = bf16[8,64,512]{2,1,0:T(8,128)(2,1)S(1)} all-to-all(bf16[8,64,512]{2,1,0:T(8,128)(2,1)S(1)} %bitcast.81), channel_id=1, replica_groups=mesh['req'=2,'ctx'=4,'tp'=4] {'req','tp'}, dimensions={0} | all-to-all | bytes 1048576 | tf_op jit(solution)/shard_map/all_to_all | solution.py:137
  239.1 0.1 convert_reduce_fusion.1
  239.2 2.7 %collective-permute-start.1 = (bf16[64,512]{1,0:T(8,128)(2,1)S(1)}, bf16[64,512]{1,0:T(8,128)(2,1)S(1)}, u32[]{:S(2)}, u32[]{:S(2)}) collective-permute-start(bf16[64,512]{1,0:T(8,128)(2,1)S(1)} %add_convert_fusion), channel_id=1, source_target_pairs={{0,0},{1,4},{2,8},{3,12},{4,1},{5,5},{6,9},{7,13},{8,2},{9,6},{10,... | collective-permute-start | bytes 196616 | tf_op jit(solution)/shard_map/ppermute | solution.py:139
  242.0 5.2 %collective-permute-done.1 = bf16[64,512]{1,0:T(8,128)(2,1)S(1)} collective-permute-done((bf16[64,512]{1,0:T(8,128)(2,1)S(1)}, bf16[64,512]{1,0:T(8,128)(2,1)S(1)}, u32[]{:S(2)}, u32[]{:S(2)}) %collective-permute-start.1) | collective-permute-done | bytes 65568 | tf_op jit(solution)/shard_map/ppermute | solution.py:139
  247.2 0.6 copy.83
  (45 shorter events, 0.3 us)
Async XLA Ops:
  6.5 42.9 %copy-start = (bf16[512,512]{1,0:T(8,128)(2,1)S(1)}, bf16[512,512]{1,0:T(8,128)(2,1)}, u32[]{:S(2)}) copy-start(bf16[512,512]{1,0:T(8,128)(2,1)} %param.21) | copy-start | bytes 1572868
  16.0 4.8 %copy-start.12 = (bf16[1,2048,1,128]{3,1,2,0:T(8,128)(2,1)S(1)}, bf16[1,2048,1,128]{3,1,2,0:T(8,128)(2,1)}, u32[]{:S(2)}) copy-start(bf16[1,2048,1,128]{3,1,2,0:T(8,128)(2,1)} %param.18) | copy-start | bytes 1572868
  16.0 4.8 %copy-start.13 = (bf16[256,1,128]{2,0,1:T(8,128)(2,1)S(1)}, bf16[256,1,128]{2,0,1:T(8,128)(2,1)}, u32[]{:S(2)}) copy-start(bf16[256,1,128]{2,0,1:T(8,128)(2,1)} %param.16) | copy-start | bytes 196612
  20.8 8.6 %copy-start.14 = (bf16[64,512]{1,0:T(8,128)(2,1)S(1)}, bf16[64,512]{1,0:T(8,128)(2,1)}, u32[]{:S(2)}) copy-start(bf16[64,512]{1,0:T(8,128)(2,1)} %param.20) | copy-start | bytes 196612
  20.8 13.0 %copy-start.10 = (s32[64,6]{0,1:T(8,128)S(1)}, s32[64,6]{0,1:T(8,128)}, u32[]{:S(2)}) copy-start(s32[64,6]{0,1:T(8,128)} %param.23) | copy-start | bytes 4612
  20.8 13.1 %copy-start.11 = (f32[64,6]{0,1:T(8,128)S(1)}, f32[64,6]{0,1:T(8,128)}, u32[]{:S(2)}) copy-start(f32[64,6]{0,1:T(8,128)} %param.24) | copy-start | bytes 4612
  25.9 17.2 %all-to-all-start = ((f32[4,136,256]{2,1,0:T(8,128)}), f32[4,136,256]{2,1,0:T(8,128)S(1)}, u32[]{:S(2)}, u32[]{:S(2)}) async-start(f32[4,136,256]{2,1,0:T(8,128)} %maximum_bitcast_fusion), calls=%async_computation | async-start | bytes 1114112 | tf_op jit(solution)/shard_map/all_to_all | solution.py:104
  29.4 41.3 %collective-permute-start = (bf16[64,512]{1,0:T(8,128)(2,1)S(1)}, bf16[64,512]{1,0:T(8,128)(2,1)S(1)}, u32[]{:S(2)}, u32[]{:S(2)}) collective-permute-start(bf16[64,512]{1,0:T(8,128)(2,1)S(1)} %copy-done.14), channel_id=1, source_target_pairs={{0,0},{1,4},{2,8},{3,12},{4,1},{5,5},{6,9},{7,13},{8,2},{9,6},{10,... | collective-permute-start | bytes 196616 | tf_op jit(solution)/shard_map/ppermute | solution.py:102
  50.5 20.1 %all-to-all-start.1 = ((f32[4,64,512]{2,1,0:T(8,128)}), f32[4,64,512]{2,1,0:T(8,128)S(1)}, u32[]{:S(2)}, u32[]{:S(2)}) async-start(f32[4,64,512]{2,1,0:T(8,128)} %bitcast.13), calls=%async_computation.1 | async-start | bytes 1048576 | tf_op jit(solution)/shard_map/all_to_all | solution.py:109
  56.2 0.6 copy-start.2
  57.4 55.8 %copy-start.4 = (s32[512,32]{0,1:T(8,128)}, s32[512,32]{0,1:T(8,128)S(1)}, u32[]{:S(2)}) copy-start(s32[512,32]{0,1:T(8,128)S(1)} %reshape.144) | copy-start | bytes 196612
  70.7 42.5 %copy-start.7 = (bf16[64,512]{1,0:T(8,128)(2,1)}, bf16[64,512]{1,0:T(8,128)(2,1)S(1)}, u32[]{:S(2)}) copy-start(bf16[64,512]{1,0:T(8,128)(2,1)S(1)} %collective-permute-done) | copy-start | bytes 196612
  129.2 5.4 %copy-start.3 = (s32[8,64,6]{1,2,0:T(8,128)S(1)}, s32[8,64,6]{1,2,0:T(8,128)}, u32[]{:S(2)}) copy-start(s32[8,64,6]{1,2,0:T(8,128)} %copy-done.2) | copy-start | bytes 36868
  129.2 5.4 %copy-start.9 = (f32[8,64,6]{1,2,0:T(8,128)S(1)}, f32[8,64,6]{1,2,0:T(8,128)}, u32[]{:S(2)}) copy-start(f32[8,64,6]{1,2,0:T(8,128)} %get-tuple-element.13) | copy-start | bytes 36868
  129.3 5.7 %copy-start.15 = (u32[32]{0:T(128)S(1)}, u32[32]{0:T(128)}, u32[]{:S(2)}) copy-start(u32[32]{0:T(128)} %constant.96) | copy-start | bytes 388
  129.3 59.5 %copy-start.5 = (s32[512,32]{0,1:T(8,128)S(1)}, s32[512,32]{0,1:T(8,128)}, u32[]{:S(2)}) copy-start(s32[512,32]{0,1:T(8,128)} %copy-done.4) | copy-start | bytes 196612
  129.3 61.1 %all-to-all-start.2 = ((bf16[4,512,2,352]{1,3,2,0:T(8,128)(2,1)}), bf16[4,512,2,352]{1,3,2,0:T(8,128)(2,1)S(1)}, u32[]{:S(2)}, u32[]{:S(2)}) async-start(bf16[4,512,2,352]{1,3,2,0:T(8,128)(2,1)} %pad_maximum_fusion), calls=%async_computation.2 | async-start | bytes 5767168 | tf_op jit(solution)/shard_map/all_to_all | solution.py:127
  134.6 74.9 %all-gather.4.cloned.1.call-start = ((), (), s32[]{:S(2)}) async-start(), calls=%async_computation.4 | async-start | bytes 1966080 | tf_op jit(solution)/shard_map/all_gather | solution.py:132
  190.8 18.7 %copy-start.6 = (s32[512,32]{0,1:T(8,128)S(1)}, s32[512,32]{0,1:T(8,128)}, u32[]{:S(2)}) copy-start(s32[512,32]{0,1:T(8,128)} %copy-done.4) | copy-start | bytes 196612
  209.5 29.7 %copy-start.8 = (bf16[64,512]{1,0:T(8,128)(2,1)S(1)}, bf16[64,512]{1,0:T(8,128)(2,1)}, u32[]{:S(2)}) copy-start(bf16[64,512]{1,0:T(8,128)(2,1)} %copy-done.7) | copy-start | bytes 196612
  209.5 38.4 %copy-start.1 = (bf16[512,512]{1,0:T(8,128)(2,1)S(1)}, bf16[512,512]{1,0:T(8,128)(2,1)}, u32[]{:S(2)}) copy-start(bf16[512,512]{1,0:T(8,128)(2,1)} %param.21) | copy-start | bytes 1572868
  239.2 8.0 %collective-permute-start.1 = (bf16[64,512]{1,0:T(8,128)(2,1)S(1)}, bf16[64,512]{1,0:T(8,128)(2,1)S(1)}, u32[]{:S(2)}, u32[]{:S(2)}) collective-permute-start(bf16[64,512]{1,0:T(8,128)(2,1)S(1)} %add_convert_fusion), channel_id=1, source_target_pairs={{0,0},{1,4},{2,8},{3,12},{4,1},{5,5},{6,9},{7,13},{8,2},{9,6},{10,... | collective-permute-start | bytes 196616 | tf_op jit(solution)/shard_map/ppermute | solution.py:139
Sparse Core Ops, SparseCore 0:
  192.7 16.7 all-gather.3
where the time goes:
time: 256 us; the launch traced here: 255 us
  blocking collectives  121 us (47%)
  matrix products  38.5 us (15%)
  waiting for transfers between devices  34.6 us (14%)
  starting transfers between devices  21.2 us (8%)
  between operations  14.5 us (6%)
  other arithmetic  14 us (5%)
  local copies, waits for them, and re-layouts  10.6 us (4%)
    psum x1, blocking collectives, body(): squares = lax.psum(squares, 'ctx')  33.5 us
    all_gather x1, blocking collectives, body(): scaled = lax.all_gather(scaled, ('req', 'tp'), tiled=True)  32.5 us
    all_to_all x1, blocking collectives, body(): mixed = lax.all_to_all(mixed, ('req', 'tp'), 0, 0, tiled=True)  21.4 us
    unnamed x1, blocking collectives  18.9 us
    all_gather x1, waiting for transfers between devices, body(): inner = lax.all_gather(inner, 'ctx', tiled=True).reshape(exp_dev, slots, -1)  17 us
    all_to_all x1, waiting for transfers between devices, body(): part = lax.all_to_all(part, 'tp', 0, 0, tiled=True)  12.4 us
    all_gather x1, blocking collectives, route_tables(): both = lax.all_gather(both, ('req', 'ctx'))  9.25 us
    dot_general x1, matrix products, body(): jnp.einsum('esd,edf->esf', rows, w_up, preferred_element_type=jnp.float32)  8.61 us
  transfers between devices with their start and end apart: 6, of which 3 were waited for; matrix products, arithmetic and copies ran while one was open for 2% of the time, Pallas kernels for 0%

commit v1 on v0

--- a/solution.py
+++ b/solution.py
@@ -114,7 +114,27 @@
     squares = lax.psum(squares, "ctx")
     factor = lax.rsqrt(squares / norm_gain.shape[0] + 1e-06)
     factor = lax.all_gather(factor, ("req", "tp"), tiled=True)
-    scaled = lax.all_gather(scaled, ("req", "tp"), tiled=True)
+    ways, here, step = (
+        lax.axis_size(("req", "tp")),
+        lax.axis_index(("req", "tp")),
+        scaled.shape[0],
+    )
+    dims = [n * ways if d == 0 else n for d, n in enumerate(scaled.shape)]
+    full = lax.dynamic_update_slice_in_dim(
+        jnp.zeros(dims, scaled.dtype), scaled, here * step, axis=0
+    )
+    going_up = going_down = scaled
+    for far in range(1, ways // 2 + 1):
+        going_up = lax.ppermute(going_up, ("req", "tp"), [(d, (d + 1) % ways) for d in range(ways)])
+        full = lax.dynamic_update_slice_in_dim(full, going_up, (here - far) % ways * step, axis=0)
+        if 2 * far < ways:
+            going_down = lax.ppermute(
+                going_down, ("req", "tp"), [(d, (d - 1) % ways) for d in range(ways)]
+            )
+            full = lax.dynamic_update_slice_in_dim(
+                full, going_down, (here + far) % ways * step, axis=0
+            )
+    scaled = full
     pick = code[:, None, :] == jnp.arange(slots, dtype=jnp.int32)[None, :, None]
     row_factor = jnp.sum(jnp.where(pick, factor, 0.0), -1, keepdims=True)
     row_gate = jnp.sum(jnp.where(pick, gate_at[:, None, :], 0.0), -1, keepdims=True)

time: 256 us -> 246 us (0.961)
  blocking collectives: 121 us -> 87.2 us
  starting transfers between devices: 21.2 us -> 38.2 us
  waiting for transfers between devices: 34.6 us -> 42.2 us
    all_gather x1 -> x0, blocking collectives: 32.5 us -> none  [body(): scaled = lax.all_gather(scaled, ('req', 'tp'), tiled=True)]
    ppermute x0 -> x7, starting transfers between devices: none -> 15.3 us  [the longest x3 15.2 us: body(): lax.ppermute(going_down, ('req', 'tp'), [(d, (d - 1) % ways) for d in ran...]
    ppermute x0 -> x7, waiting for transfers between devices: none -> 12.1 us  [the longest x4 11.4 us: body(): lax.ppermute(going_up, ('req', 'tp'), [(d, (d + 1) % ways) for d in range...]
    all_to_all x1, waiting for transfers between devices: 12.4 us -> 4.51 us  [body(): part = lax.all_to_all(part, 'tp', 0, 0, tiled=True)]
  transfers between devices with their start and end apart: 6 -> 13, of which waited for: 3 -> 11; matrix products, arithmetic and copies ran while one was open for 2% -> 3% of each run, Pallas kernels for 0% -> 0%
where the time goes in v1:
time: 246 us; the launch traced here: 245 us
  blocking collectives  87.2 us (35%)
  waiting for transfers between devices  42.2 us (17%)
  matrix products  38.5 us (16%)
  starting transfers between devices  38.2 us (16%)
  between operations  14.7 us (6%)
  other arithmetic  14 us (6%)
  local copies, waits for them, and re-layouts  10.5 us (4%)
    psum x1, blocking collectives, body(): squares = lax.psum(squares, 'ctx')  33.4 us
    all_to_all x1, blocking collectives, body(): mixed = lax.all_to_all(mixed, ('req', 'tp'), 0, 0, tiled=True)  21.3 us
    all_gather x1, waiting for transfers between devices, body(): inner = lax.all_gather(inner, 'ctx', tiled=True).reshape(exp_dev, slots, -1)  18.3 us
    unnamed x1, blocking collectives  17.4 us
    ppermute x3, starting transfers between devices, body(): lax.ppermute(going_down, ('req', 'tp'), [(d, (d - 1) % ways) for d in ran...  15.2 us
    ppermute x4, waiting for transfers between devices, body(): lax.ppermute(going_up, ('req', 'tp'), [(d, (d + 1) % ways) for d in range...  11.4 us
    all_gather x1, blocking collectives, route_tables(): both = lax.all_gather(both, ('req', 'ctx'))  9.25 us
    dot_general x1, matrix products, body(): jnp.einsum('esd,edf->esf', rows, w_gate, preferred_element_type=jnp.float32)  8.61 us
  transfers between devices with their start and end apart: 13, of which 11 were waited for; matrix products, arithmetic and copies ran while one was open for 3% of the time, Pallas kernels for 0%

profile of v1, /device:TPU:4, one launch (start us, length us, event | category | flops | bytes accessed | tf_op | source)
XLA Modules:
  0.0 245.4 jit_solution(7524411711137591661)
XLA Ops:
  6.6 1.0 copy.55
  7.6 1.2 dynamic_slice.10
  8.9 0.7 add_compare_fusion
  9.5 6.5 %fusion = (f32[1024]{0:T(1024)S(1)}, f32[2304,1024]{1,0:T(8,128)S(1)}) fusion(s32[1024]{0:T(1024)S(1)} %fusion.38, s32[2304]{0:T(1024)S(1)} %iota_add_fusion, pred[2304]{0:T(1024)(128)(4,1)S(1)} %get-tuple-element.17, pred[2304]{0:T(1024)(128)(4,1)S(1)} %get-tuple-element.18, pred[]{:T(512)S(6)} %eq.39, bf16[1024,128]{1,0:T(8,128)(2,1)S(1)} %bitcast.83, ...), kind=kOutput, calls=%fused_computation.3 | convolution fusion | flops 619314176 | bytes 10311169 | tf_op jit(solution)/shard_map/dot_general | solution.py:21
  16.0 4.7 %fusion.1 = f32[1024]{0:T(1024)S(1)} fusion(f32[2304,1024]{1,0:T(8,128)S(1)} %get-tuple-element.16, f32[1024]{0:T(1024)S(1)} %get-tuple-element.15, s32[1024]{0:T(1024)S(1)} %fusion.38, s32[2304]{0:T(1024)S(1)} %iota_add_fusion, pred[2304]{0:T(1024)(128)(4,1)S(1)} %get-tuple-element.17, pred[2304]{0:T(1024)(128)(4,1)S(1)} %get-tuple-element.18, pred[]{:T(512)S(6)} %eq.39), kind=kLoop, calls=%fused_computation.5 | loop fusion | flops 18873344 | bytes 9463297 | tf_op jit(solution)/shard_map/reduce_sum | solution.py:33
  20.8 4.0 %fusion.3 = f32[128,1024]{1,0:T(8,128)S(1)} fusion(f32[2304,1024]{1,0:T(8,128)S(1)} %get-tuple-element.16, f32[1024]{0:T(1024)S(1)} %get-tuple-element.15, s32[1024]{0:T(1024)S(1)} %fusion.38, s32[2304]{0:T(1024)S(1)} %iota_add_fusion, pred[2304]{0:T(1024)(128)(4,1)S(1)} %get-tuple-element.17, pred[2304]{0:T(1024)(128)(4,1)S(1)} %get-tuple-element.18, ...), kind=kOutput, calls=%fused_computation.7 | convolution fusion | flops 624033792 | bytes 10573313 | tf_op jit(solution)/shard_map/dot_general | solution.py:34
  24.9 0.1 pad.7.clone
  25.0 0.9 maximum_bitcast_fusion
  25.9 3.5 %all-to-all-start = ((f32[4,136,256]{2,1,0:T(8,128)}), f32[4,136,256]{2,1,0:T(8,128)S(1)}, u32[]{:S(2)}, u32[]{:S(2)}) async-start(f32[4,136,256]{2,1,0:T(8,128)} %maximum_bitcast_fusion), calls=%async_computation | async-start | bytes 1114112 | tf_op jit(solution)/shard_map/all_to_all | solution.py:104
  29.4 4.5 %collective-permute-start = (bf16[64,512]{1,0:T(8,128)(2,1)S(1)}, bf16[64,512]{1,0:T(8,128)(2,1)S(1)}, u32[]{:S(2)}, u32[]{:S(2)}) collective-permute-start(bf16[64,512]{1,0:T(8,128)(2,1)S(1)} %copy-done.15), channel_id=1, source_target_pairs={{0,0},{1,4},{2,8},{3,12},{4,1},{5,5},{6,9},{7,13},{8,2},{9,6},{10,... | collective-permute-start | bytes 196616 | tf_op jit(solution)/shard_map/ppermute | solution.py:102
  33.9 0.8 dynamic_slice.11
  34.6 2.2 all-to-all-done
  36.9 0.1 copy.59
  37.0 0.1 div.31
  37.1 0.1 copy_bitcast_fusion.1
  37.2 5.8 %all_gather.15 = bf16[256,512]{1,0:T(8,128)(2,1)S(1)} all-gather(bf16[64,512]{1,0:T(8,128)(2,1)S(1)} %copy_bitcast_fusion.1), channel_id=1, replica_groups=mesh['req'=2,'ctx'=4,'tp'=4] {'ctx'}, dimensions={0}, use_global_device_ids=true | all-gather | bytes 327680 | tf_op jit(solution)/shard_map/all_gather | solution.py:106
  43.0 1.1 fusion.53
  44.1 6.9 %all-to-all-start.1 = ((f32[4,64,512]{2,1,0:T(8,128)}), f32[4,64,512]{2,1,0:T(8,128)S(1)}, u32[]{:S(2)}, u32[]{:S(2)}) async-start(f32[4,64,512]{2,1,0:T(8,128)} %bitcast.13), calls=%async_computation.1 | async-start | bytes 1048576 | tf_op jit(solution)/shard_map/all_to_all | solution.py:109
  51.1 9.3 %all-gather.1 = f32[8,64,12]{1,2,0:T(8,128)S(1)} all-gather(f32[1,64,12]{1,2,0:T(8,128)S(1)} %maximum_bitcast_fusion.1), channel_id=2, replica_groups=mesh['req'=2,'ctx'=4,'tp'=4] {'req','ctx'}, dimensions={0}, use_global_device_ids=true | all-gather | bytes 27648 | tf_op jit(solution)/shard_map/all_gather | solution.py:56
  60.3 0.6 fusion.52
  61.0 0.2 compare_reduce_fusion
  61.1 0.4 copy-done.5
  61.6 4.5 %all-to-all-done.1 = f32[4,64,512]{2,1,0:T(8,128)S(1)} async-done(((f32[4,64,512]{2,1,0:T(8,128)}), f32[4,64,512]{2,1,0:T(8,128)S(1)}, u32[]{:S(2)}, u32[]{:S(2)}) %all-to-all-start.1) | async-done | bytes 524320 | tf_op jit(solution)/shard_map/all_to_all | solution.py:109
  66.3 4.7 %collective-permute-start.2 = (bf16[64,512]{1,0:T(8,128)(2,1)S(1)}, bf16[64,512]{1,0:T(8,128)(2,1)S(1)}, u32[]{:S(2)}, u32[]{:S(2)}) collective-permute-start(bf16[64,512]{1,0:T(8,128)(2,1)S(1)} %get-tuple-element.8), channel_id=1, source_target_pairs={{0,19},{1,0},{2,1},{3,2},{16,3},{17,16},{18,17},{19,18},{4,23},{5,... | collective-permute-start | bytes 196616 | tf_op jit(solution)/shard_map/ppermute | solution.py:131
  71.0 0.2 fusion.13
  71.3 0.1 copy.61
  71.4 0.1 reshape.144
  71.6 1.7 collective-permute-done.1
  73.2 0.1 collective-permute-done.2
  73.3 5.3 %collective-permute-start.4 = (bf16[64,512]{1,0:T(8,128)(2,1)S(1)}, bf16[64,512]{1,0:T(8,128)(2,1)S(1)}, u32[]{:S(2)}, u32[]{:S(2)}) collective-permute-start(bf16[64,512]{1,0:T(8,128)(2,1)S(1)} %collective-permute-done.2), channel_id=1, source_target_pairs={{0,19},{1,0},{2,1},{3,2},{16,3},{17,16},{18,17},{19,18},{4,23},{5,... | collective-permute-start | bytes 196616 | tf_op jit(solution)/shard_map/ppermute | solution.py:131
  78.6 1.7 collective-permute-done.3
  80.3 0.2 collective-permute-done.4
  80.5 5.2 %collective-permute-start.6 = (bf16[64,512]{1,0:T(8,128)(2,1)S(1)}, bf16[64,512]{1,0:T(8,128)(2,1)S(1)}, u32[]{:S(2)}, u32[]{:S(2)}) collective-permute-start(bf16[64,512]{1,0:T(8,128)(2,1)S(1)} %collective-permute-done.4), channel_id=1, source_target_pairs={{0,19},{1,0},{2,1},{3,2},{16,3},{17,16},{18,17},{19,18},{4,23},{5,... | collective-permute-start | bytes 196616 | tf_op jit(solution)/shard_map/ppermute | solution.py:131
  85.8 1.5 collective-permute-done.5
  87.3 0.4 collective-permute-done.6
  87.6 6.6 %collective-permute-done.7 = bf16[64,512]{1,0:T(8,128)(2,1)S(1)} collective-permute-done((bf16[64,512]{1,0:T(8,128)(2,1)S(1)}, bf16[64,512]{1,0:T(8,128)(2,1)S(1)}, u32[]{:S(2)}, u32[]{:S(2)}) %collective-permute-start.7) | collective-permute-done | bytes 65568 | tf_op jit(solution)/shard_map/ppermute | solution.py:128
  94.2 1.3 fusion.6
  95.5 8.6 %convolution_convert_fusion.1 = bf16[32,64,352]{2,1,0:T(8,128)(2,1)} fusion(bf16[32,64,512]{2,1,0:T(8,128)(2,1)S(1)} %fusion.6, bf16[32,512,352]{1,2,0:T(8,128)(2,1)} %param.25), kind=kOutput, calls=%fused_computation.18 | convolution fusion | flops 738918400 | bytes 15073280 | tf_op jit(solution)/shard_map/esd,edf->esf/dot_general | solution.py:143
  104.1 2.5 %copy.62 = bf16[4,512,1,352]{1,3,2,0:T(8,128)(2,1)} copy(bf16[4,512,1,352]{3,1,0,2:T(8,128)(2,1)} %bitcast.77) | data formatting | bytes 2883584 | tf_op jit(solution)/shard_map/stack | solution.py:145
  106.7 8.6 %convolution_convert_fusion = bf16[32,64,352]{2,1,0:T(8,128)(2,1)} fusion(bf16[32,64,512]{2,1,0:T(8,128)(2,1)S(1)} %fusion.6, bf16[32,512,352]{1,2,0:T(8,128)(2,1)} %param.26), kind=kOutput, calls=%fused_computation.17 | convolution fusion | flops 738918400 | bytes 15073280 | tf_op jit(solution)/shard_map/esd,edf->esf/dot_general | solution.py:144
  115.3 1.7 copy.63
  117.0 3.2 %pad_maximum_fusion = bf16[4,512,2,352]{1,3,2,0:T(8,128)(2,1)} fusion(bf16[4,512,1,352]{1,3,2,0:T(8,128)(2,1)S(1)} %copy.63, bf16[4,512,1,352]{1,3,2,0:T(8,128)(2,1)} %copy.62), kind=kLoop, calls=%fused_computation.14 | loop fusion | flops 1441792 | bytes 5767168 | tf_op jit(solution)/shard_map/stack | solution.py:145
  120.2 5.3 %all-to-all-start.2 = ((bf16[4,512,2,352]{1,3,2,0:T(8,128)(2,1)}), bf16[4,512,2,352]{1,3,2,0:T(8,128)(2,1)S(1)}, u32[]{:S(2)}, u32[]{:S(2)}) async-start(bf16[4,512,2,352]{1,3,2,0:T(8,128)(2,1)} %pad_maximum_fusion), calls=%async_computation.2 | async-start | bytes 5767168 | tf_op jit(solution)/shard_map/all_to_all | solution.py:147
  125.5 0.2 fusion.14
  125.7 0.1 copy.67
  125.8 0.1 reshape.146
  125.9 0.7 dynamic-slice
  127.3 0.1 multiply_reduce_fusion
  127.4 33.4 %psum.7 = f32[64]{0:T(128)S(1)} all-reduce(f32[64]{0:T(128)S(1)} %multiply_reduce_fusion), channel_id=1, replica_groups=mesh['req'=2,'ctx'=4,'tp'=4] {'ctx'}, use_global_device_ids=true, to_apply=%region_9.10 | all-reduce | flops 64 | bytes 512 | tf_op jit(solution)/shard_map/psum | solution.py:114
  160.7 0.1 rsqrt_dynamic-update-slice_fusion
  160.8 17.4 %all-reduce = f32[512]{0:T(512)S(1)} all-reduce(f32[512]{0:T(512)S(1)} %rsqrt_dynamic-update-slice_fusion), channel_id=1, replica_groups=mesh['req'=2,'ctx'=4,'tp'=4] {'req','tp'}, use_global_device_ids=true, to_apply=%add | all-reduce | flops 512 | bytes 4096
  178.3 1.5 select_reduce_fusion
  179.8 0.1 reshape_broadcast_in_dim.3
  179.9 0.4 convert_reduce_fusion
  180.3 0.1 fusion.51
  180.4 0.3 copy.72
  180.7 0.3 copy.73
  181.0 1.0 fusion.16
  182.0 18.3 %all-gather.4.cloned.1.call-done = bf16[2048,352]{1,0:T(8,128)(2,1)} async-done(((bf16[512,352]{1,0:T(8,128)(2,1)}), bf16[2048,352]{1,0:T(8,128)(2,1)}) %all-gather.4.cloned.1.call-update) | async-done | bytes 1441808 | tf_op jit(solution)/shard_map/all_gather | solution.py:152
  200.3 8.2 %fusion.10 = bf16[512,512]{1,0:T(8,128)(2,1)S(1)} fusion(s32[32,512]{1,0:T(8,128)S(1)} %bitcast.86, bf16[32,64,352]{2,1,0:T(8,128)(2,1)} %bitcast.92, bf16[32,352,512]{2,1,0:T(8,128)(2,1)} %param.27, f32[32,64]{1,0:T(8,128)S(1)} %get-tuple-element.5), kind=kOutput, calls=%fused_computation.20 | convolution fusion | flops 1815347200 | bytes 13574144 | tf_op jit(solution)/shard_map/est,esd->td/dot_general | solution.py:155
  208.6 21.3 %all_to_all.20 = bf16[8,64,512]{2,1,0:T(8,128)(2,1)S(1)} all-to-all(bf16[8,64,512]{2,1,0:T(8,128)(2,1)S(1)} %bitcast.81), channel_id=1, replica_groups=mesh['req'=2,'ctx'=4,'tp'=4] {'req','tp'}, dimensions={0} | all-to-all | bytes 1048576 | tf_op jit(solution)/shard_map/all_to_all | solution.py:157
  230.0 2.8 %collective-permute-start.8 = (bf16[64,512]{1,0:T(8,128)(2,1)S(1)}, bf16[64,512]{1,0:T(8,128)(2,1)S(1)}, u32[]{:S(2)}, u32[]{:S(2)}) collective-permute-start(bf16[64,512]{1,0:T(8,128)(2,1)S(1)} %add_convert_fusion), channel_id=1, source_target_pairs={{0,0},{1,4},{2,8},{3,12},{4,1},{5,5},{6,9},{7,13},{8,2},{9,6},{10,... | collective-permute-start | bytes 196616 | tf_op jit(solution)/shard_map/ppermute | solution.py:159
  232.8 5.2 %collective-permute-done.8 = bf16[64,512]{1,0:T(8,128)(2,1)S(1)} collective-permute-done((bf16[64,512]{1,0:T(8,128)(2,1)S(1)}, bf16[64,512]{1,0:T(8,128)(2,1)S(1)}, u32[]{:S(2)}, u32[]{:S(2)}) %collective-permute-start.8) | collective-permute-done | bytes 65568 | tf_op jit(solution)/shard_map/ppermute | solution.py:159
  237.9 0.6 copy.91
  (69 shorter events, 0.6 us)
Async XLA Ops:
  6.5 36.5 %copy-start = (bf16[512,512]{1,0:T(8,128)(2,1)S(1)}, bf16[512,512]{1,0:T(8,128)(2,1)}, u32[]{:S(2)}) copy-start(bf16[512,512]{1,0:T(8,128)(2,1)} %param.21) | copy-start | bytes 1572868
  16.0 4.8 %copy-start.13 = (bf16[1,2048,1,128]{3,1,2,0:T(8,128)(2,1)S(1)}, bf16[1,2048,1,128]{3,1,2,0:T(8,128)(2,1)}, u32[]{:S(2)}) copy-start(bf16[1,2048,1,128]{3,1,2,0:T(8,128)(2,1)} %param.18) | copy-start | bytes 1572868
  16.0 4.8 %copy-start.14 = (bf16[256,1,128]{2,0,1:T(8,128)(2,1)S(1)}, bf16[256,1,128]{2,0,1:T(8,128)(2,1)}, u32[]{:S(2)}) copy-start(bf16[256,1,128]{2,0,1:T(8,128)(2,1)} %param.16) | copy-start | bytes 196612
  20.8 8.6 %copy-start.15 = (bf16[64,512]{1,0:T(8,128)(2,1)S(1)}, bf16[64,512]{1,0:T(8,128)(2,1)}, u32[]{:S(2)}) copy-start(bf16[64,512]{1,0:T(8,128)(2,1)} %param.20) | copy-start | bytes 196612
  20.8 13.1 %copy-start.11 = (s32[64,6]{0,1:T(8,128)S(1)}, s32[64,6]{0,1:T(8,128)}, u32[]{:S(2)}) copy-start(s32[64,6]{0,1:T(8,128)} %param.23) | copy-start | bytes 4612
  24.8 26.2 %copy-start.12 = (f32[64,6]{0,1:T(8,128)S(1)}, f32[64,6]{0,1:T(8,128)}, u32[]{:S(2)}) copy-start(f32[64,6]{0,1:T(8,128)} %param.24) | copy-start | bytes 4612
  25.9 10.9 %all-to-all-start = ((f32[4,136,256]{2,1,0:T(8,128)}), f32[4,136,256]{2,1,0:T(8,128)S(1)}, u32[]{:S(2)}, u32[]{:S(2)}) async-start(f32[4,136,256]{2,1,0:T(8,128)} %maximum_bitcast_fusion), calls=%async_computation | async-start | bytes 1114112 | tf_op jit(solution)/shard_map/all_to_all | solution.py:104
  29.4 36.8 %collective-permute-start = (bf16[64,512]{1,0:T(8,128)(2,1)S(1)}, bf16[64,512]{1,0:T(8,128)(2,1)S(1)}, u32[]{:S(2)}, u32[]{:S(2)}) collective-permute-start(bf16[64,512]{1,0:T(8,128)(2,1)S(1)} %copy-done.15), channel_id=1, source_target_pairs={{0,0},{1,4},{2,8},{3,12},{4,1},{5,5},{6,9},{7,13},{8,2},{9,6},{10,... | collective-permute-start | bytes 196616 | tf_op jit(solution)/shard_map/ppermute | solution.py:102
  44.1 21.9 %all-to-all-start.1 = ((f32[4,64,512]{2,1,0:T(8,128)}), f32[4,64,512]{2,1,0:T(8,128)S(1)}, u32[]{:S(2)}, u32[]{:S(2)}) async-start(f32[4,64,512]{2,1,0:T(8,128)} %bitcast.13), calls=%async_computation.1 | async-start | bytes 1048576 | tf_op jit(solution)/shard_map/all_to_all | solution.py:109
  61.0 0.6 copy-start.5
  66.1 28.1 %copy-start.2 = (bf16[64,512]{1,0:T(8,128)(2,1)}, bf16[64,512]{1,0:T(8,128)(2,1)S(1)}, u32[]{:S(2)}) copy-start(bf16[64,512]{1,0:T(8,128)(2,1)S(1)} %collective-permute-done) | copy-start | bytes 196612
  66.2 7.0 %collective-permute-start.1 = (bf16[64,512]{1,0:T(8,128)(2,1)S(1)}, bf16[64,512]{1,0:T(8,128)(2,1)S(1)}, u32[]{:S(2)}, u32[]{:S(2)}) collective-permute-start(bf16[64,512]{1,0:T(8,128)(2,1)S(1)} %get-tuple-element.8), channel_id=1, source_target_pairs={{0,1},{1,2},{2,3},{3,16},{16,17},{17,18},{18,19},{19,0},{4,5},{5,6... | collective-permute-start | bytes 196616 | tf_op jit(solution)/shard_map/ppermute | solution.py:128
  66.3 7.0 %collective-permute-start.2 = (bf16[64,512]{1,0:T(8,128)(2,1)S(1)}, bf16[64,512]{1,0:T(8,128)(2,1)S(1)}, u32[]{:S(2)}, u32[]{:S(2)}) collective-permute-start(bf16[64,512]{1,0:T(8,128)(2,1)S(1)} %get-tuple-element.8), channel_id=1, source_target_pairs={{0,19},{1,0},{2,1},{3,2},{16,3},{17,16},{18,17},{19,18},{4,23},{5,... | collective-permute-start | bytes 196616 | tf_op jit(solution)/shard_map/ppermute | solution.py:131
  71.5 32.6 %copy-start.7 = (s32[512,32]{0,1:T(8,128)}, s32[512,32]{0,1:T(8,128)S(1)}, u32[]{:S(2)}) copy-start(s32[512,32]{0,1:T(8,128)S(1)} %reshape.144) | copy-start | bytes 196612
  73.2 7.1 %collective-permute-start.3 = (bf16[64,512]{1,0:T(8,128)(2,1)S(1)}, bf16[64,512]{1,0:T(8,128)(2,1)S(1)}, u32[]{:S(2)}, u32[]{:S(2)}) collective-permute-start(bf16[64,512]{1,0:T(8,128)(2,1)S(1)} %collective-permute-done.1), channel_id=1, source_target_pairs={{0,1},{1,2},{2,3},{3,16},{16,17},{17,18},{18,19},{19,0},{4,5},{5,6... | collective-permute-start | bytes 196616 | tf_op jit(solution)/shard_map/ppermute | solution.py:128
  73.3 7.2 %collective-permute-start.4 = (bf16[64,512]{1,0:T(8,128)(2,1)S(1)}, bf16[64,512]{1,0:T(8,128)(2,1)S(1)}, u32[]{:S(2)}, u32[]{:S(2)}) collective-permute-start(bf16[64,512]{1,0:T(8,128)(2,1)S(1)} %collective-permute-done.2), channel_id=1, source_target_pairs={{0,19},{1,0},{2,1},{3,2},{16,3},{17,16},{18,17},{19,18},{4,23},{5,... | collective-permute-start | bytes 196616 | tf_op jit(solution)/shard_map/ppermute | solution.py:131
  80.3 7.0 %collective-permute-start.5 = (bf16[64,512]{1,0:T(8,128)(2,1)S(1)}, bf16[64,512]{1,0:T(8,128)(2,1)S(1)}, u32[]{:S(2)}, u32[]{:S(2)}) collective-permute-start(bf16[64,512]{1,0:T(8,128)(2,1)S(1)} %collective-permute-done.3), channel_id=1, source_target_pairs={{0,1},{1,2},{2,3},{3,16},{16,17},{17,18},{18,19},{19,0},{4,5},{5,6... | collective-permute-start | bytes 196616 | tf_op jit(solution)/shard_map/ppermute | solution.py:128
  80.5 7.1 %collective-permute-start.6 = (bf16[64,512]{1,0:T(8,128)(2,1)S(1)}, bf16[64,512]{1,0:T(8,128)(2,1)S(1)}, u32[]{:S(2)}, u32[]{:S(2)}) collective-permute-start(bf16[64,512]{1,0:T(8,128)(2,1)S(1)} %collective-permute-done.4), channel_id=1, source_target_pairs={{0,19},{1,0},{2,1},{3,2},{16,3},{17,16},{18,17},{19,18},{4,23},{5,... | collective-permute-start | bytes 196616 | tf_op jit(solution)/shard_map/ppermute | solution.py:131
  87.3 7.0 %collective-permute-start.7 = (bf16[64,512]{1,0:T(8,128)(2,1)S(1)}, bf16[64,512]{1,0:T(8,128)(2,1)S(1)}, u32[]{:S(2)}, u32[]{:S(2)}) collective-permute-start(bf16[64,512]{1,0:T(8,128)(2,1)S(1)} %collective-permute-done.5), channel_id=1, source_target_pairs={{0,1},{1,2},{2,3},{3,16},{16,17},{17,18},{18,19},{19,0},{4,5},{5,6... | collective-permute-start | bytes 196616 | tf_op jit(solution)/shard_map/ppermute | solution.py:128
  120.2 5.4 %copy-start.6 = (s32[8,64,6]{1,2,0:T(8,128)S(1)}, s32[8,64,6]{1,2,0:T(8,128)}, u32[]{:S(2)}) copy-start(s32[8,64,6]{1,2,0:T(8,128)} %copy-done.5) | copy-start | bytes 36868
  120.2 5.4 %copy-start.10 = (f32[8,64,6]{1,2,0:T(8,128)S(1)}, f32[8,64,6]{1,2,0:T(8,128)}, u32[]{:S(2)}) copy-start(f32[8,64,6]{1,2,0:T(8,128)} %get-tuple-element.13) | copy-start | bytes 36868
  120.2 5.7 %copy-start.16 = (u32[32]{0:T(128)S(1)}, u32[32]{0:T(128)}, u32[]{:S(2)}) copy-start(u32[32]{0:T(128)} %constant.145) | copy-start | bytes 388
  120.2 7.0 %copy-start.3 = (bf16[64,512]{1,0:T(8,128)(2,1)S(1)}, bf16[64,512]{1,0:T(8,128)(2,1)}, u32[]{:S(2)}) copy-start(bf16[64,512]{1,0:T(8,128)(2,1)} %copy-done.2) | copy-start | bytes 196612
  120.2 58.1 %copy-start.8 = (s32[512,32]{0,1:T(8,128)S(1)}, s32[512,32]{0,1:T(8,128)}, u32[]{:S(2)}) copy-start(s32[512,32]{0,1:T(8,128)} %copy-done.7) | copy-start | bytes 196612
  120.2 59.6 %all-to-all-start.2 = ((bf16[4,512,2,352]{1,3,2,0:T(8,128)(2,1)}), bf16[4,512,2,352]{1,3,2,0:T(8,128)(2,1)S(1)}, u32[]{:S(2)}, u32[]{:S(2)}) async-start(bf16[4,512,2,352]{1,3,2,0:T(8,128)(2,1)} %pad_maximum_fusion), calls=%async_computation.2 | async-start | bytes 5767168 | tf_op jit(solution)/shard_map/all_to_all | solution.py:147
  125.5 74.8 %all-gather.4.cloned.1.call-start = ((), (), s32[]{:S(2)}) async-start(), calls=%async_computation.4 | async-start | bytes 1966080 | tf_op jit(solution)/shard_map/all_gather | solution.py:152
  180.3 20.0 %copy-start.9 = (s32[512,32]{0,1:T(8,128)S(1)}, s32[512,32]{0,1:T(8,128)}, u32[]{:S(2)}) copy-start(s32[512,32]{0,1:T(8,128)} %copy-done.7) | copy-start | bytes 196612
  200.3 29.6 %copy-start.4 = (bf16[64,512]{1,0:T(8,128)(2,1)S(1)}, bf16[64,512]{1,0:T(8,128)(2,1)}, u32[]{:S(2)}) copy-start(bf16[64,512]{1,0:T(8,128)(2,1)} %copy-done.2) | copy-start | bytes 196612
  200.3 38.3 %copy-start.1 = (bf16[512,512]{1,0:T(8,128)(2,1)S(1)}, bf16[512,512]{1,0:T(8,128)(2,1)}, u32[]{:S(2)}) copy-start(bf16[512,512]{1,0:T(8,128)(2,1)} %param.21) | copy-start | bytes 1572868
  230.0 8.0 %collective-permute-start.8 = (bf16[64,512]{1,0:T(8,128)(2,1)S(1)}, bf16[64,512]{1,0:T(8,128)(2,1)S(1)}, u32[]{:S(2)}, u32[]{:S(2)}) collective-permute-start(bf16[64,512]{1,0:T(8,128)(2,1)S(1)} %add_convert_fusion), channel_id=1, source_target_pairs={{0,0},{1,4},{2,8},{3,12},{4,1},{5,5},{6,9},{7,13},{8,2},{9,6},{10,... | collective-permute-start | bytes 196616 | tf_op jit(solution)/shard_map/ppermute | solution.py:159
Sparse Core Ops, SparseCore 0:
  182.2 18.1 all-gather.3
